TPU v7x, 32 devices: a whole 2x2x4 slice. The times are simulated.
32 devices in a mesh: ia: 4 (over z), ja: 2 (over y), ka: 4 (over x, core).
Axes of the slice: x: 2, y: 2, z: 4, core: 2. Of those that a mesh axis runs over, the one named last changes fastest.
Arguments:
- tile_values: bfloat16 [768, 128], P(('ia', 'ja', 'ka')), may hold values from -0.59765625 to 0.59765625
- tile_rows: int32 [768, 128], P(('ia', 'ja', 'ka')), may hold values from 0 to 63
- tile_cols: int32 [768, 128], P(('ia', 'ja', 'ka')), may hold values from 0 to 2047
- tile_depths: int32 [768, 128], P(('ia', 'ja', 'ka')), may hold values from 0 to 1023
- tile_live: int32 [32, 8], P(('ia', 'ja', 'ka')), may hold values from 0 to 3, as said below
- factor_b: bfloat16 [16, 2, 2048], P(None, 'ja', ('ia', 'ka')), may hold values from -6 to 6
- factor_c: bfloat16 [16, 4, 1024], P(None, 'ka', ('ia', 'ja')), may hold values from -6 to 6
- proj: float32 [16, 256], replicated, may hold values from -0.375 to 0.375
Outputs:
- tucker_y: float32 [2048, 256], P(('ia', 'ja', 'ka'))
- gram: float32 [256, 256], replicated
- new_factor: float32 [16, 2048], P(None, ('ia', 'ja', 'ka'))
Inputs may be any that keep to these rules, and one draw needn't show every extreme that they name: tile_live[d, o] counts the live leading slots among the 3 slots that device d holds for the device at index o along ja+ka within its mode-1 block; in every draw there is an owner for which every device has all 3 slots live, and every device has some owner with all 3 slots live.
All inputs are finite; a program needn't handle non-finite values.
Results may differ from a plain program's by a relative error of at most 0.0041.
Values may be sent and summed in bfloat16 or wider, within the bound.
A program may use at most 64 MiB of HBM per device.

v0:
```python
import jax
import jax.numpy as jnp
from jax import lax
from jax.sharding import PartitionSpec as P

RANK = 16
ROWS_DEV = 64


def owner_block(scaled, depth_rows, target):
    kron_rows = (scaled[:, None] * depth_rows[None, :]).reshape(
        scaled.shape[0] * depth_rows.shape[0], -1
    )
    onehot = (target.reshape(1, -1) == lax.iota(jnp.int32, ROWS_DEV)[:, None]).astype(jnp.bfloat16)
    return lax.dot_general(
        onehot, kron_rows, (((1,), (1,)), ((), ())), preferred_element_type=jnp.float32
    )


def group_blocks(scaled, depth_rows, target, begin_slot, pair_size, slot_count):
    rank_size = scaled.shape[0]
    tile_width = scaled.shape[2]
    scaled_part = lax.dynamic_slice_in_dim(scaled, begin_slot, pair_size * slot_count, 1)
    depth_part = lax.dynamic_slice_in_dim(depth_rows, begin_slot, pair_size * slot_count, 1)
    target_part = lax.dynamic_slice_in_dim(target, begin_slot, pair_size * slot_count, 0)
    scaled_part = scaled_part.reshape(rank_size, pair_size, slot_count, tile_width)
    depth_part = depth_part.reshape(depth_rows.shape[0], pair_size, slot_count, tile_width)
    target_part = target_part.reshape(pair_size, slot_count, tile_width)
    return jax.vmap(owner_block, in_axes=(1, 1, 0))(scaled_part, depth_part, target_part)


def owner_total(scaled, depth_rows, target, groups, slot_count):
    pair_size = 2
    columns = scaled.shape[0] * depth_rows.shape[0]
    result = jnp.zeros((ROWS_DEV, columns), jnp.float32)

    def turn(turn_index, result):
        begin_slot = turn_index * pair_size * slot_count
        blocks = group_blocks(scaled, depth_rows, target, begin_slot, pair_size, slot_count)
        return result + jnp.sum(blocks, axis=0)

    return lax.fori_loop(0, groups // pair_size, turn, result)


def on_device(tile_values, tile_rows, tile_cols, tile_depths, tile_live, factor_b, factor_c, proj):
    owners = lax.axis_size("ja") * lax.axis_size("ka")
    slot_total = tile_values.shape[0]
    slot_count = slot_total // owners
    mode_two = lax.all_gather(factor_b, ("ia", "ka"), axis=2, tiled=True)[:, 0, :]
    mode_three = lax.all_gather(factor_c, ("ia", "ja"), axis=2, tiled=True)[:, 0, :]
    slot_index = lax.iota(jnp.int32, slot_total)
    owner_of = slot_index // slot_count
    counts = jnp.sum(
        jnp.where(owner_of[:, None] == lax.iota(jnp.int32, owners)[None, :], tile_live, 0), axis=1
    )
    is_live = slot_index % slot_count < counts
    target = jnp.where(is_live[:, None], tile_rows, ROWS_DEV)
    scaled = (
        tile_values.astype(jnp.float32)[None]
        * jnp.take(mode_two, tile_cols, axis=1).astype(jnp.float32)
    ).astype(jnp.bfloat16)
    depth_rows = jnp.take(mode_three, tile_depths, axis=1)
    payload = jnp.concatenate([scaled, depth_rows], axis=0)
    arrived, routed = (
        lax.all_to_all(payload, ("ja", "ka"), split_axis=1, concat_axis=1, tiled=True),
        lax.all_to_all(target[None], ("ja", "ka"), split_axis=1, concat_axis=1, tiled=True),
    )
    summed = owner_total(arrived[:RANK], arrived[RANK:], routed[0], owners, slot_count)
    local_gram = lax.dot_general(
        summed,
        summed,
        (((0,), (0,)), ((), ())),
        precision=lax.Precision.HIGHEST,
        preferred_element_type=jnp.float32,
    )
    gram_total = lax.psum(local_gram, ("ia", "ja", "ka"))
    gram = gram_total / (ROWS_DEV * owners * lax.axis_size("ia"))
    new_factor = lax.dot_general(
        proj,
        summed,
        (((1,), (1,)), ((), ())),
        precision=lax.Precision.HIGHEST,
        preferred_element_type=jnp.float32,
    )
    return (summed, gram, new_factor)


def solution(mesh):
    return jax.shard_map(
        on_device,
        mesh=mesh,
        in_specs=(
            P(("ia", "ja", "ka"), None),
            P(("ia", "ja", "ka"), None),
            P(("ia", "ja", "ka"), None),
            P(("ia", "ja", "ka"), None),
            P(("ia", "ja", "ka"), None),
            P(None, "ja", ("ia", "ka")),
            P(None, "ka", ("ia", "ja")),
            P(),
        ),
        out_specs=(P(("ia", "ja", "ka"), None), P(), P(None, ("ia", "ja", "ka"))),
        check_vma=False,
    )
```

profile of v0, /device:TPU:0, one launch (start us, length us, event | category | flops | bytes accessed | tf_op | source)
XLA Modules:
  0.0 239.9 jit_solution(6678735856828618585)
XLA Ops:
  7.2 0.0 copy-start
  7.2 0.0 copy-start.2
  7.2 0.8 bitcast_clamp_fusion.1
  8.0 0.0 copy-done.2
  8.0 0.7 copy-done.3
  8.7 0.7 copy-done.6
  9.4 0.1 copy.29
  9.5 24.6 %all_gather.6 = bf16[16,1,2048]{0,2,1:T(8,128)(2,1)S(1)} all-gather(bf16[16,1,128]{0,2,1:T(8,128)(2,1)S(1)} %copy.29), channel_id=1, replica_groups=mesh['ia'=4,'ja'=2,'ka'=4] {'ia','ka'}, dimensions={2}, use_global_device_ids=true | all-gather | bytes 69632 | tf_op jit(solution)/shard_map/all_gather | solution.py:49
  34.1 9.2 %gather_fusion = bf16[3072,16]{1,0:T(8,128)(2,1)S(1)} fusion(bf16[16,2048]{0,1:T(8,128)(2,1)S(1)} %bitcast.41, s32[3072]{0:T(1024)S(1)} %bitcast_clamp_fusion.1), kind=kCustom, calls=%fused_computation | custom fusion | bytes 208896 | tf_op jit(solution)/shard_map/jit(_take)/gather | solution.py:60
  43.3 0.0 copy-start.5
  43.3 0.3 copy.30
  43.5 0.4 copy-done.5
  44.0 0.7 copy-done.7
  44.6 0.1 copy.31
  44.8 30.8 %all_gather.7 = bf16[16,1,1024]{0,2,1:T(8,128)(2,1)S(1)} all-gather(bf16[16,1,128]{0,2,1:T(8,128)(2,1)S(1)} %copy.31), channel_id=1, replica_groups=mesh['ia'=4,'ja'=2,'ka'=4] {'ia','ja'}, dimensions={2}, use_global_device_ids=true | all-gather | bytes 36864 | tf_op jit(solution)/shard_map/all_gather | solution.py:50
  75.5 9.2 %gather_fusion.1 = bf16[3072,16]{1,0:T(8,128)(2,1)S(1)} fusion(bf16[16,1024]{0,1:T(8,128)(2,1)S(1)} %bitcast.40, s32[3072]{0:T(1024)S(1)} %bitcast_clamp_fusion), kind=kCustom, calls=%fused_computation.1 | custom fusion | bytes 208896 | tf_op jit(solution)/shard_map/jit(_take)/gather | solution.py:62
  84.7 0.3 copy.32
  85.0 0.7 pad_maximum_fusion
  85.7 3.5 %all-to-all-start.1 = ((bf16[32,24,128]{2,0,1:T(8,128)(2,1)}), bf16[32,24,128]{2,0,1:T(8,128)(2,1)S(1)}, u32[]{:S(2)}, u32[]{:S(2)}) async-start(bf16[32,24,128]{2,0,1:T(8,128)(2,1)} %pad_maximum_fusion), calls=%async_computation.1 | async-start | bytes 393216 | tf_op jit(solution)/shard_map/all_to_all | solution.py:65
  89.3 0.0 copy-start.8
  89.3 0.6 copy-done.8
  90.0 0.1 select_reduce_fusion
  90.1 0.0 copy-done.4
  90.1 0.7 broadcast_select_fusion
  90.7 4.7 %all-to-all-done.1 = bf16[32,24,128]{2,0,1:T(8,128)(2,1)S(1)} async-done(((bf16[32,24,128]{2,0,1:T(8,128)(2,1)}), bf16[32,24,128]{2,0,1:T(8,128)(2,1)S(1)}, u32[]{:S(2)}, u32[]{:S(2)}) %all-to-all-start.1) | async-done | bytes 196640 | tf_op jit(solution)/shard_map/all_to_all | solution.py:65
  95.4 3.3 %all-to-all-start = ((s32[1,24,128]{2,0,1:T(1,128)}), s32[1,24,128]{2,0,1:T(1,128)S(1)}, u32[]{:S(2)}, u32[]{:S(2)}) async-start(s32[1,24,128]{2,0,1:T(1,128)} %bitcast.1), calls=%async_computation | async-start | bytes 24576 | tf_op jit(solution)/shard_map/all_to_all | solution.py:66
  98.7 0.0 all-reduce.2.cloned.1.call-start
  98.8 4.6 %all-to-all-done = s32[1,24,128]{2,0,1:T(1,128)S(1)} async-done(((s32[1,24,128]{2,0,1:T(1,128)}), s32[1,24,128]{2,0,1:T(1,128)S(1)}, u32[]{:S(2)}, u32[]{:S(2)}) %all-to-all-start) | async-done | bytes 12320 | tf_op jit(solution)/shard_map/all_to_all | solution.py:66
  103.4 3.7 %while.16 = (s32[]{:T(128)}, f32[64,256]{1,0:T(8,128)S(1)}, s32[24,128]{1,0:T(8,128)S(1)}, bf16[16,24,128]{2,0,1:T(8,128)(2,1)S(1)}, bf16[16,24,128]{2,0,1:T(8,1...) while((s32[]{:T(128)}, f32[64,256]{1,0:T(8,128)S(1)}, s32[24,128]{1,0:T(8,128)S(1)}, ...), condition=%wide.region_2.3_spmd.clone, body=%wide.region_1.2_spmd.clone.sunk | while | flops 25444360 | bytes 1965213 | solution.py:42
  103.5 0.2 broadcast_multiply_fusion.3
  103.7 0.3 mul.80
  104.0 0.3 fusion.14
  104.4 0.2 broadcast_multiply_fusion.3
  104.6 0.3 mul.80
  105.0 0.3 fusion.14
  105.3 0.2 broadcast_multiply_fusion.3
  105.5 0.3 mul.80
  105.9 0.3 fusion.14
  106.3 0.2 broadcast_multiply_fusion.3
  106.5 0.3 mul.80
  106.9 0.3 fusion.14
  107.1 0.0 copy-start.1
  107.2 1.1 fusion.5
  108.3 0.0 all-reduce.2.cloned.1.call-update
  108.3 0.0 copy-done.1
  108.3 0.8 convolution_bitcast_fusion.1
  109.1 122.3 %all-reduce.2.cloned.1.call-done = f32[256,256]{1,0:T(8,128)} async-done(((f32[256,256]{1,0:T(8,128)}), f32[256,256]{1,0:T(8,128)}) %all-reduce.2.cloned.1.call-update) | async-done | bytes 262160 | tf_op jit(solution)/shard_map/psum | solution.py:76
  231.4 1.7 broadcast_multiply_fusion.1
  (35 shorter events, 0.4 us)
Async XLA Ops:
  7.2 101.2 %copy-start = (f32[16,256]{1,0:T(8,128)S(1)}, f32[16,256]{1,0:T(8,128)}, u32[]{:S(2)}) copy-start(f32[16,256]{1,0:T(8,128)} %param.17) | copy-start | bytes 49156
  7.2 0.8 copy-start.2
  8.0 0.7 copy-start.3
  8.7 0.7 copy-start.6
  43.3 0.7 copy-start.5
  44.0 0.7 copy-start.7
  85.7 4.3 %copy-start.4 = (s32[24,128]{1,0:T(8,128)S(1)}, s32[24,128]{1,0:T(8,128)}, u32[]{:S(2)}) copy-start(s32[24,128]{1,0:T(8,128)} %param.11) | copy-start | bytes 36868
  85.7 9.7 %all-to-all-start.1 = ((bf16[32,24,128]{2,0,1:T(8,128)(2,1)}), bf16[32,24,128]{2,0,1:T(8,128)(2,1)S(1)}, u32[]{:S(2)}, u32[]{:S(2)}) async-start(bf16[32,24,128]{2,0,1:T(8,128)(2,1)} %pad_maximum_fusion), calls=%async_computation.1 | async-start | bytes 393216 | tf_op jit(solution)/shard_map/all_to_all | solution.py:65
  89.3 0.7 copy-start.8
  95.4 8.0 %all-to-all-start = ((s32[1,24,128]{2,0,1:T(1,128)}), s32[1,24,128]{2,0,1:T(1,128)S(1)}, u32[]{:S(2)}, u32[]{:S(2)}) async-start(s32[1,24,128]{2,0,1:T(1,128)} %bitcast.1), calls=%async_computation | async-start | bytes 24576 | tf_op jit(solution)/shard_map/all_to_all | solution.py:66
  98.7 132.6 %all-reduce.2.cloned.1.call-start = ((), (), s32[]{:S(2)}) async-start(), calls=%async_computation.2 | async-start | bytes 524288 | tf_op jit(solution)/shard_map/psum | solution.py:76
  107.1 1.2 copy-start.1
Sparse Core Ops, SparseCore 0:
  108.4 122.9 all-reduce.1
where the time goes:
time: 240 us
  waiting for transfers between devices  132 us (55%)
  blocking collectives  55.4 us (23%)
  local copies, waits for them, and re-layouts  23.8 us (10%)
  between operations  14.2 us (6%)
  starting transfers between devices  6.9 us (3%)
  other arithmetic  4.78 us (2%)
  matrix products  2.98 us (1%)
    psum x1, waiting for transfers between devices, on_device(): gram_total = lax.psum(local_gram, ('ia', 'ja', 'ka'))  122 us
    all_gather x1, blocking collectives, on_device(): lax.all_gather(factor_c, ('ia', 'ja'), axis=2, tiled=True)[:, 0, :]  30.8 us
    all_gather x1, blocking collectives, on_device(): lax.all_gather(factor_b, ('ia', 'ka'), axis=2, tiled=True)[:, 0, :]  24.6 us
    gather x2, local copies, waits for them, and re-layouts, on_device(): depth_rows = jnp.take(mode_three, tile_depths, axis=1)  9.41 us
    gather x2, local copies, waits for them, and re-layouts, on_device(): jnp.take(mode_two, tile_cols, axis=1).astype(jnp.float32)  9.41 us
  transfers between devices with their start and end apart: 3, of which 3 were waited for; matrix products, arithmetic and copies ran while one was open for 1% of the time, Pallas kernels for 0%

commit v1 on v0

v1 whole, which is shorter than its diff:
```python
import functools

import jax
import jax.numpy as jnp
from jax import lax
from jax.experimental import pallas as pl
from jax.experimental.pallas import tpu as pltpu
from jax.sharding import PartitionSpec as P

ROWS_DEV = 64
LANES = 128
MESH = pl.DeviceIdType.MESH


def repeat(count, body, init):
    if count <= 16:
        for step in range(count):
            init = body(step, init)
        return init
    group = 8

    def turn(index, carry):
        for step in range(group):
            carry = body(index * group + step, carry)
        return carry

    return lax.fori_loop(0, count // group, turn, init)


def lookup(table, index):
    chunks, rank, _ = table.shape
    high = jnp.broadcast_to(index // LANES, (rank, LANES))
    low = jnp.broadcast_to(index % LANES, (rank, LANES))

    def step(chunk, found):
        here = jnp.take_along_axis(table[chunk], low, axis=1, mode="promise_in_bounds")
        return jnp.where(high == chunk, here, found)

    return repeat(chunks, step, jnp.zeros((rank, LANES), jnp.float32))


def kernel(
    n_ia, n_ja, n_ka,
    values, rows, cols, depths, live, fb, fc, proj,
    y_out, gram_out, nf_out,
    values_v, rows_v, cols_v, depths_v, proj_v, live_s, scale_v,
    tb_in, tc_in, tb, tc,
    rows_send, rows_recv, pay_send, pay_recv, kron,
    g_own, g_send, g_recv, z_send, z_recv, final,
    load_sem, tb_ssem, tb_rsem, tc_ssem, tc_rsem, rows_ssem, rows_rsem, pay_ssem, pay_rsem,
    g_ssem, g_rsem, z_ssem, z_rsem, f_ssem, f_rsem,
):
    owners = n_ja * n_ka
    slots = values.shape[0] // owners
    rank = fb.shape[0]
    a, b, c = lax.axis_index("ia"), lax.axis_index("ja"), lax.axis_index("ka")
    me_b = a * n_ka + c
    me_c = a * n_ja + b
    me_o = b * n_ka + c

    loads = []
    for index, (src, dst) in enumerate((
        (values, values_v), (rows, rows_v), (cols, cols_v), (depths, depths_v),
        (proj, proj_v), (live, live_s), (fb, tb_in.at[me_b]), (fc, tc_in.at[me_c]),
    )):
        loads.append(pltpu.make_async_copy(src, dst, load_sem.at[index]))
        loads[-1].start()

    def b_peer(j):
        peer = lax.rem(me_b + j, n_ia * n_ka)
        return (peer // n_ka, b, lax.rem(peer, n_ka))

    def c_peer(j):
        peer = lax.rem(me_c + j, n_ia * n_ja)
        return (peer // n_ja, lax.rem(peer, n_ja), c)

    def o_peer(j):
        peer = lax.rem(me_o + j, owners)
        return (a, peer // n_ka, lax.rem(peer, n_ka))

    def a_peer(j):
        return (lax.rem(a + j, n_ia), b, c)

    barrier = pltpu.get_barrier_semaphore()
    for count, peer in ((n_ia * n_ka, b_peer), (n_ia * n_ja, c_peer), (owners, o_peer)):
        @pl.loop(1, count)
        def _(j, peer=peer):
            pl.semaphore_signal(barrier, inc=1, device_id=peer(j), device_id_type=MESH)
    pl.semaphore_wait(barrier, n_ia * n_ka + n_ia * n_ja + owners - 3)

    def remote(src, dst, ssem, rsem, peer):
        return pltpu.make_async_remote_copy(
            src_ref=src, dst_ref=dst, send_sem=ssem, recv_sem=rsem,
            device_id=peer, device_id_type=MESH,
        )

    def tb_copy(j, slot):
        return remote(fb, tb_in.at[slot], tb_ssem.at[j], tb_rsem.at[slot], b_peer(j))

    def tc_copy(j, slot):
        return remote(fc, tc_in.at[slot], tc_ssem.at[j], tc_rsem.at[slot], c_peer(j))

    @pl.loop(1, n_ia * n_ka)
    def _(j):
        tb_copy(j, me_b).start()

    @pl.loop(1, n_ia * n_ja)
    def _(j):
        tc_copy(j, me_c).start()

    for load in loads:
        load.wait()

    def rows_copy(j, slot):
        return remote(
            rows_send.at[lax.rem(me_o + j, owners)], rows_recv.at[slot],
            rows_ssem.at[j], rows_rsem.at[slot], o_peer(j),
        )

    def pay_copy(j, slot):
        return remote(
            pay_send.at[lax.rem(me_o + j, owners)], pay_recv.at[slot],
            pay_ssem.at[j], pay_rsem.at[slot], o_peer(j),
        )

    @pl.loop(0, owners)
    def _(o):
        for t in range(slots):
            rows_send[o, pl.ds(t, 1), :] = rows_v[pl.ds(o * slots + t, 1), :]

    @pl.loop(1, owners)
    def _(j):
        rows_copy(j, me_o).start()

    scale_v[...] = values_v[...].astype(jnp.float32)
    tb[me_b] = tb_in[me_b].astype(jnp.float32)
    tc[me_c] = tc_in[me_c].astype(jnp.float32)

    @pl.loop(1, n_ia * n_ka)
    def _(j):
        slot = lax.rem(me_b + n_ia * n_ka - j, n_ia * n_ka)
        tb_copy(j, slot).wait_recv()
        tb[slot] = tb_in[slot].astype(jnp.float32)

    @pl.loop(1, n_ia * n_ja)
    def _(j):
        slot = lax.rem(me_c + n_ia * n_ja - j, n_ia * n_ja)
        tc_copy(j, slot).wait_recv()
        tc[slot] = tc_in[slot].astype(jnp.float32)

    def fill(o):
        count = live_s[0, o]
        for t in range(slots):
            row = pl.ds(o * slots + t, 1)
            value = jnp.where(count > t, scale_v[row, :], 0.0)
            pay_send[o, t, pl.ds(0, rank), :] = (lookup(tb, cols_v[row, :]) * value).astype(jnp.bfloat16)
            pay_send[o, t, pl.ds(rank, rank), :] = lookup(tc, depths_v[row, :]).astype(jnp.bfloat16)

    @pl.loop(1, owners)
    def _(j):
        fill(lax.rem(me_o + j, owners))
        pay_copy(j, me_o).start()

    fill(me_o)

    def block(payload, target):
        hot = []
        for t in range(slots):
            part = payload[t].astype(jnp.float32)
            depth = part[rank:]
            for p in range(rank):
                kron[pl.ds(p * rank, rank), pl.ds(t * LANES, LANES)] = (
                    part[p:p + 1] * depth
                ).astype(jnp.bfloat16)
            spot = lax.broadcasted_iota(jnp.int32, (ROWS_DEV, LANES), 0)
            hot.append((target[pl.ds(t, 1), :] == spot).astype(jnp.float32).astype(jnp.bfloat16))
        return lax.dot_general(
            jnp.concatenate(hot, axis=1), kron[...], (((1,), (1,)), ((), ())),
            preferred_element_type=jnp.float32,
        )

    y_out[...] = block(pay_send.at[me_o], rows_send.at[me_o])

    @pl.loop(1, owners)
    def _(j):
        slot = lax.rem(me_o + owners - j, owners)
        rows_copy(j, slot).wait_recv()
        pay_copy(j, slot).wait_recv()
        y_out[...] += block(pay_recv.at[slot], rows_recv.at[slot])

    y = y_out[...]
    gram = lax.dot_general(
        y, y, (((0,), (0,)), ((), ())),
        precision=lax.Precision.HIGHEST, preferred_element_type=jnp.float32,
    ) * (1.0 / (ROWS_DEV * owners * n_ia))
    g_own[...] = gram.reshape(g_own.shape)
    g_send[...] = gram.reshape(g_own.shape).astype(jnp.bfloat16)

    def g_copy(j, slot):
        return remote(
            g_send.at[lax.rem(me_o + j, owners)], g_recv.at[slot],
            g_ssem.at[j], g_rsem.at[slot], o_peer(j),
        )

    @pl.loop(1, owners)
    def _(j):
        g_copy(j, me_o).start()

    nf_out[...] = lax.dot_general(
        proj_v[...], y, (((1,), (1,)), ((), ())),
        precision=lax.Precision.HIGHEST, preferred_element_type=jnp.float32,
    )

    total = g_own[me_o]
    for j in range(1, owners):
        slot = lax.rem(me_o + owners - j, owners)
        g_copy(j, slot).wait_recv()
        total = total + g_recv[slot].astype(jnp.float32)
    z_send[...] = total.astype(jnp.bfloat16)
    z_recv[a] = total.astype(jnp.bfloat16)

    def z_copy(j, slot):
        return remote(z_send, z_recv.at[slot], z_ssem.at[j], z_rsem.at[slot], a_peer(j))

    for j in range(1, n_ia):
        z_copy(j, a).start()
    for j in range(1, n_ia):
        z_copy(j, lax.rem(a + n_ia - j, n_ia)).wait_recv()
    total = z_recv[0].astype(jnp.float32)
    for index in range(1, n_ia):
        total = total + z_recv[index].astype(jnp.float32)
    final[me_o] = total.astype(jnp.bfloat16)

    def f_copy(j, slot):
        return remote(final.at[slot], final.at[slot], f_ssem.at[j], f_rsem.at[slot], o_peer(j))

    height = z_send.shape[0]

    def put(slot):
        start = pl.multiple_of(slot * height, height)
        gram_out[pl.ds(start, height), :] = final[slot].astype(jnp.float32)

    @pl.loop(1, owners)
    def _(j):
        f_copy(j, me_o).start()

    put(me_o)

    @pl.loop(1, owners)
    def _(j):
        slot = lax.rem(me_o + owners - j, owners)
        f_copy(j, slot).wait_recv()
        put(slot)

    @pl.loop(1, n_ia * n_ka)
    def _(j):
        tb_copy(j, me_b).wait_send()

    @pl.loop(1, n_ia * n_ja)
    def _(j):
        tc_copy(j, me_c).wait_send()

    @pl.loop(1, owners)
    def _(j):
        rows_copy(j, me_o).wait_send()
        pay_copy(j, me_o).wait_send()
        g_copy(j, me_o).wait_send()
        f_copy(j, me_o).wait_send()

    for j in range(1, n_ia):
        z_copy(j, a).wait_send()


def on_device(tile_values, tile_rows, tile_cols, tile_depths, tile_live, factor_b, factor_c, proj):
    n_ia, n_ja, n_ka = (lax.axis_size(name) for name in ("ia", "ja", "ka"))
    owners = n_ja * n_ka
    slot_total, tile = tile_values.shape
    slots = slot_total // owners
    rank = factor_b.shape[0]
    columns = proj.shape[1]
    height = columns // owners
    chunks_b, chunks_c = n_ia * n_ka, n_ia * n_ja
    vmem, dma = pltpu.VMEM, pltpu.SemaphoreType.DMA
    f32, bf16, i32 = jnp.float32, jnp.bfloat16, jnp.int32
    return pl.pallas_call(
        functools.partial(kernel, n_ia, n_ja, n_ka),
        out_shape=(
            jax.ShapeDtypeStruct((ROWS_DEV, columns), f32),
            jax.ShapeDtypeStruct((columns, columns), f32),
            jax.ShapeDtypeStruct((rank, ROWS_DEV), f32),
        ),
        in_specs=[pl.BlockSpec(memory_space=pl.ANY)] * 8,
        out_specs=tuple([pl.BlockSpec(memory_space=pltpu.VMEM)] * 3),
        scratch_shapes=[
            vmem((slot_total, tile), bf16),
            vmem((slot_total, tile), i32),
            vmem((slot_total, tile), i32),
            vmem((slot_total, tile), i32),
            vmem(proj.shape, f32),
            pltpu.SMEM((1, owners), i32),
            vmem((slot_total, tile), f32),
            vmem((chunks_b, rank, LANES), bf16),
            vmem((chunks_c, rank, LANES), bf16),
            vmem((chunks_b, rank, LANES), f32),
            vmem((chunks_c, rank, LANES), f32),
            vmem((owners, slots, tile), i32),
            vmem((owners, slots, tile), i32),
            vmem((owners, slots, 2 * rank, tile), bf16),
            vmem((owners, slots, 2 * rank, tile), bf16),
            vmem((columns, slots * tile), bf16),
            vmem((owners, height, columns), f32),
            vmem((owners, height, columns), bf16),
            vmem((owners, height, columns), bf16),
            vmem((height, columns), bf16),
            vmem((n_ia, height, columns), bf16),
            vmem((owners, height, columns), bf16),
            dma((8,)),
            dma((chunks_b,)), dma((chunks_b,)),
            dma((chunks_c,)), dma((chunks_c,)),
            dma((owners,)), dma((owners,)),
            dma((owners,)), dma((owners,)),
            dma((owners,)), dma((owners,)),
            dma((n_ia,)), dma((n_ia,)),
            dma((owners,)), dma((owners,)),
        ],
        compiler_params=pltpu.CompilerParams(collective_id=0, has_side_effects=True),
    )(
        tile_values, tile_rows, tile_cols, tile_depths, tile_live,
        factor_b[:, 0, :], factor_c[:, 0, :], proj,
    )


def solution(mesh):
    return jax.shard_map(
        on_device,
        mesh=mesh,
        in_specs=(
            P(("ia", "ja", "ka"), None),
            P(("ia", "ja", "ka"), None),
            P(("ia", "ja", "ka"), None),
            P(("ia", "ja", "ka"), None),
            P(("ia", "ja", "ka"), None),
            P(None, "ja", ("ia", "ka")),
            P(None, "ka", ("ia", "ja")),
            P(),
        ),
        out_specs=(P(("ia", "ja", "ka"), None), P(), P(None, ("ia", "ja", "ka"))),
        check_vma=False,
    )
```

time: 240 us -> 34.7 us (0.14)
  waiting for transfers between devices: 132 us -> 0 us
  blocking collectives: 55.4 us -> 0 us
  Pallas kernels: 0 us -> 30.1 us
  local copies, waits for them, and re-layouts: 23.8 us -> 3.76 us
  between operations: 14.2 us -> 0.64 us
  starting transfers between devices: 6.9 us -> 0 us
  other arithmetic: 4.78 us -> 0 us
  matrix products: 2.98 us -> 0 us
    psum x1 -> x0, waiting for transfers between devices: 122 us -> none  [on_device(): gram_total = lax.psum(local_gram, ('ia', 'ja', 'ka'))]
    all_gather x2 -> x0, blocking collectives: 55.4 us -> none  [the longest x1 30.8 us: on_device(): lax.all_gather(factor_c, ('ia', 'ja'), axis=2, tiled=True)[:, 0, :]]
    pallas_call x0 -> x1, Pallas kernels: none -> 30.1 us  [on_device(): pl.pallas_call(functools.partial(kernel, n_ia, n_ja, n_ka), out_shape=(ja...]
    gather x4 -> x0, local copies, waits for them, and re-layouts: 18.8 us -> none  [the longest x2 9.41 us: on_device(): depth_rows = jnp.take(mode_three, tile_depths, axis=1)]
    all_to_all x2 -> x0, waiting for transfers between devices: 9.27 us -> none  [the longest x1 4.68 us: on_device(): lax.all_to_all(payload, ('ja', 'ka'), split_axis=1, concat_axis=1, tiled=...]
    all_to_all x2 -> x0, starting transfers between devices: 6.86 us -> none  [the longest x1 3.52 us: on_device(): lax.all_to_all(payload, ('ja', 'ka'), split_axis=1, concat_axis=1, tiled=...]
    dot_general x6 -> x0, matrix products: 2.98 us -> none  [the longest x1 1.12 us: on_device(): lax.dot_general(summed, summed, (((0,), (0,)), ((), ())), precision=lax.P...]
  transfers between devices with their start and end apart: 3 -> 0, of which waited for: 3 -> 0; matrix products, arithmetic and copies ran while one was open for 1% -> 0% of each run, Pallas kernels for 0% -> 0%
where the time goes in v1:
time: 34.7 us; the launch traced here: 34.5 us
  Pallas kernels  30.1 us (87%)
  local copies, waits for them, and re-layouts  3.76 us (11%)
  between operations  0.64 us (2%)
    pallas_call x1, Pallas kernels, on_device(): pl.pallas_call(functools.partial(kernel, n_ia, n_ja, n_ka), out_shape=(ja...  30.1 us
    unnamed x5, local copies, waits for them, and re-layouts  3.76 us

profile of v1, /device:TPU:0, one launch (start us, length us, event | category | flops | bytes accessed | tf_op | source)
XLA Modules:
  0.0 34.5 jit_solution(15016571117783504077)
XLA Ops:
  0.6 30.1 %shard_map.103 = (f32[64,256]{1,0:T(8,128)}, f32[256,256]{1,0:T(8,128)}, f32[16,64]{1,0:T(8,128)}) custom-call(bf16[24,128]{1,0:T(8,128)(2,1)} %values.1, s32[24,128]{1,0:T(8,128)} %rows.1, s32[24,128]{1,0:T(8,128)} %cols.1, s32[24,128]{1,0:T(8,128)} %depths.1, s32[1,8]{1,0:T(1,128)} %live.1, bf16[16,128]{1,0:T(8,128)(2,1)} %bitcast.2, ...), custom_call_target="tpu_custom_call" | custom-call | tf_op jit(solution)/shard_map/pallas_call | solution.py:285
  30.8 1.5 %copy.14 = f32[64,256]{1,0:T(8,128)} copy(f32[64,256]{1,0:T(8,128)} %get-tuple-element.6) | data formatting | bytes 131072
  32.2 0.0 copy-start
  32.2 1.7 %copy.15 = f32[256,256]{1,0:T(8,128)} copy(f32[256,256]{1,0:T(8,128)} %get-tuple-element.7) | data formatting | bytes 524288
  33.9 0.0 copy-done
  33.9 0.6 %copy.16 = f32[16,64]{1,0:T(8,128)} copy(f32[16,64]{1,0:T(8,128)S(1)} %copy-done) | data formatting | bytes 8192
Async XLA Ops:
  32.2 1.7 %copy-start = (f32[16,64]{1,0:T(8,128)S(1)}, f32[16,64]{1,0:T(8,128)}, u32[]{:S(2)}) copy-start(f32[16,64]{1,0:T(8,128)} %get-tuple-element.8) | copy-start | bytes 12292

commit v2 on v1

--- a/solution.py
+++ b/solution.py
@@ -29,8 +29,8 @@
 
 def lookup(table, index):
     chunks, rank, _ = table.shape
-    high = jnp.broadcast_to(index // LANES, (rank, LANES))
-    low = jnp.broadcast_to(index % LANES, (rank, LANES))
+    high = jnp.broadcast_to(lax.shift_right_logical(index, LANES.bit_length() - 1), (rank, LANES))
+    low = jnp.broadcast_to(index & (LANES - 1), (rank, LANES))
 
     def step(chunk, found):
         here = jnp.take_along_axis(table[chunk], low, axis=1, mode="promise_in_bounds")
@@ -42,11 +42,11 @@
 def kernel(
     n_ia, n_ja, n_ka,
     values, rows, cols, depths, live, fb, fc, proj,
-    y_out, gram_out, nf_out,
+    y_out, nf_out, final,
     values_v, rows_v, cols_v, depths_v, proj_v, live_s, scale_v,
     tb_in, tc_in, tb, tc,
     rows_send, rows_recv, pay_send, pay_recv, kron,
-    g_own, g_send, g_recv, z_send, z_recv, final,
+    yt_v, g_own, g_send, g_recv, z_send, z_recv,
     load_sem, tb_ssem, tb_rsem, tc_ssem, tc_rsem, rows_ssem, rows_rsem, pay_ssem, pay_rsem,
     g_ssem, g_rsem, z_ssem, z_rsem, f_ssem, f_rsem,
 ):
@@ -175,100 +175,134 @@
             spot = lax.broadcasted_iota(jnp.int32, (ROWS_DEV, LANES), 0)
             hot.append((target[pl.ds(t, 1), :] == spot).astype(jnp.float32).astype(jnp.bfloat16))
         return lax.dot_general(
-            jnp.concatenate(hot, axis=1), kron[...], (((1,), (1,)), ((), ())),
+            kron[...], jnp.concatenate(hot, axis=1), (((1,), (1,)), ((), ())),
             preferred_element_type=jnp.float32,
         )
 
-    y_out[...] = block(pay_send.at[me_o], rows_send.at[me_o])
+    yt_v[...] = block(pay_send.at[me_o], rows_send.at[me_o])
+
+    @pl.loop(1, n_ia * n_ka)
+    def _(j):
+        tb_copy(j, me_b).wait_send()
+
+    @pl.loop(1, n_ia * n_ja)
+    def _(j):
+        tc_copy(j, me_c).wait_send()
+
+    @pl.loop(1, owners)
+    def _(j):
+        rows_copy(j, me_o).wait_send()
 
     @pl.loop(1, owners)
     def _(j):
         slot = lax.rem(me_o + owners - j, owners)
         rows_copy(j, slot).wait_recv()
         pay_copy(j, slot).wait_recv()
-        y_out[...] += block(pay_recv.at[slot], rows_recv.at[slot])
-
-    y = y_out[...]
-    gram = lax.dot_general(
-        y, y, (((0,), (0,)), ((), ())),
-        precision=lax.Precision.HIGHEST, preferred_element_type=jnp.float32,
-    ) * (1.0 / (ROWS_DEV * owners * n_ia))
-    g_own[...] = gram.reshape(g_own.shape)
-    g_send[...] = gram.reshape(g_own.shape).astype(jnp.bfloat16)
-
-    def g_copy(j, slot):
+        yt_v[...] += block(pay_recv.at[slot], rows_recv.at[slot])
+
+    def g_copy(i, j, slot):
         return remote(
-            g_send.at[lax.rem(me_o + j, owners)], g_recv.at[slot],
-            g_ssem.at[j], g_rsem.at[slot], o_peer(j),
-        )
-
-    @pl.loop(1, owners)
-    def _(j):
-        g_copy(j, me_o).start()
+            g_send.at[i, lax.rem(me_o + j, owners)], g_recv.at[i, slot],
+            g_ssem.at[i, j], g_rsem.at[i, slot], o_peer(j),
+        )
+
+    def z_copy(i, j, slot):
+        return remote(z_send.at[i], z_recv.at[i, slot], z_ssem.at[i, j], z_rsem.at[i, slot], a_peer(j))
+
+    def f_copy(i, j, slot):
+        return remote(
+            final.at[i, slot], final.at[i, slot], f_ssem.at[i, j], f_rsem.at[i, slot], o_peer(j)
+        )
+
+    half = kron.shape[0] // 2
+    pieces = ((0, 0), (0, 1), (1, 1))
+    scale = 1.0 / (ROWS_DEV * owners * n_ia)
+    for i, (left, right) in enumerate(pieces):
+        piece = lax.dot_general(
+            yt_v[pl.ds(left * half, half), :], yt_v[pl.ds(right * half, half), :],
+            (((1,), (1,)), ((), ())),
+            precision=lax.Precision.HIGHEST, preferred_element_type=jnp.float32,
+        ) * scale
+        g_own[i] = piece.reshape(g_own.shape[1:])
+        g_send[i] = piece.reshape(g_own.shape[1:]).astype(jnp.bfloat16)
+
+        @pl.loop(1, owners)
+        def _(j, i=i):
+            g_copy(i, j, me_o).start()
 
     nf_out[...] = lax.dot_general(
-        proj_v[...], y, (((1,), (1,)), ((), ())),
+        proj_v[...], yt_v[...], (((1,), (0,)), ((), ())),
         precision=lax.Precision.HIGHEST, preferred_element_type=jnp.float32,
     )
-
-    total = g_own[me_o]
-    for j in range(1, owners):
-        slot = lax.rem(me_o + owners - j, owners)
-        g_copy(j, slot).wait_recv()
-        total = total + g_recv[slot].astype(jnp.float32)
-    z_send[...] = total.astype(jnp.bfloat16)
-    z_recv[a] = total.astype(jnp.bfloat16)
-
-    def z_copy(j, slot):
-        return remote(z_send, z_recv.at[slot], z_ssem.at[j], z_rsem.at[slot], a_peer(j))
-
-    for j in range(1, n_ia):
-        z_copy(j, a).start()
-    for j in range(1, n_ia):
-        z_copy(j, lax.rem(a + n_ia - j, n_ia)).wait_recv()
-    total = z_recv[0].astype(jnp.float32)
-    for index in range(1, n_ia):
-        total = total + z_recv[index].astype(jnp.float32)
-    final[me_o] = total.astype(jnp.bfloat16)
-
-    def f_copy(j, slot):
-        return remote(final.at[slot], final.at[slot], f_ssem.at[j], f_rsem.at[slot], o_peer(j))
-
-    height = z_send.shape[0]
-
-    def put(slot):
-        start = pl.multiple_of(slot * height, height)
-        gram_out[pl.ds(start, height), :] = final[slot].astype(jnp.float32)
-
-    @pl.loop(1, owners)
-    def _(j):
-        f_copy(j, me_o).start()
-
-    put(me_o)
-
-    @pl.loop(1, owners)
-    def _(j):
-        slot = lax.rem(me_o + owners - j, owners)
-        f_copy(j, slot).wait_recv()
-        put(slot)
-
-    @pl.loop(1, n_ia * n_ka)
-    def _(j):
-        tb_copy(j, me_b).wait_send()
-
-    @pl.loop(1, n_ia * n_ja)
-    def _(j):
-        tc_copy(j, me_c).wait_send()
-
-    @pl.loop(1, owners)
-    def _(j):
-        rows_copy(j, me_o).wait_send()
+    y_out[...] = jnp.transpose(yt_v[...])
+
+    @pl.loop(1, owners)
+    def _(j):
         pay_copy(j, me_o).wait_send()
-        g_copy(j, me_o).wait_send()
-        f_copy(j, me_o).wait_send()
-
-    for j in range(1, n_ia):
-        z_copy(j, a).wait_send()
+
+    for i in range(len(pieces)):
+        total = g_own[i, me_o]
+        for j in range(1, owners):
+            slot = lax.rem(me_o + owners - j, owners)
+            g_copy(i, j, slot).wait_recv()
+            total = total + g_recv[i, slot].astype(jnp.float32)
+        z_send[i] = total.astype(jnp.bfloat16)
+        z_recv[i, a] = total.astype(jnp.bfloat16)
+        for j in range(1, n_ia):
+            z_copy(i, j, a).start()
+
+    for i in range(len(pieces)):
+        for j in range(1, n_ia):
+            z_copy(i, j, lax.rem(a + n_ia - j, n_ia)).wait_recv()
+        total = z_recv[i, 0].astype(jnp.float32)
+        for index in range(1, n_ia):
+            total = total + z_recv[i, index].astype(jnp.float32)
+        final[i, me_o] = total.astype(jnp.bfloat16)
+
+        @pl.loop(1, owners)
+        def _(j, i=i):
+            f_copy(i, j, me_o).start()
+
+    @pl.loop(1, owners)
+    def _(j):
+        for i in range(len(pieces)):
+            g_copy(i, j, me_o).wait_send()
+
+    for i in range(len(pieces)):
+        for j in range(1, n_ia):
+            z_copy(i, j, a).wait_send()
+
+    @pl.loop(1, owners)
+    def _(j):
+        for i in range(len(pieces)):
+            f_copy(i, j, lax.rem(me_o + owners - j, owners)).wait_recv()
+
+    @pl.loop(1, owners)
+    def _(j):
+        for i in range(len(pieces)):
+            f_copy(i, j, me_o).wait_send()
+
+
+def finish(y, nf, final, y_out, gram_out, nf_out, gram_v, sem):
+    copies = [
+        pltpu.make_async_copy(y, y_out, sem.at[0]),
+        pltpu.make_async_copy(nf, nf_out, sem.at[1]),
+    ]
+    for copy in copies:
+        copy.start()
+    half = gram_v.shape[1] // 2
+    blocks = [final[i].astype(jnp.float32).reshape(half, half) for i in range(3)]
+    top, bottom = pl.ds(0, half), pl.ds(half, half)
+    gram_v[top, top] = blocks[0]
+    gram_v[top, bottom] = blocks[1]
+    copies.append(pltpu.make_async_copy(gram_v.at[top], gram_out.at[top], sem.at[2]))
+    copies[-1].start()
+    gram_v[bottom, top] = jnp.transpose(blocks[1])
+    gram_v[bottom, bottom] = blocks[2]
+    copies.append(pltpu.make_async_copy(gram_v.at[bottom], gram_out.at[bottom], sem.at[3]))
+    copies[-1].start()
+    for copy in copies:
+        copy.wait()
 
 
 def on_device(tile_values, tile_rows, tile_cols, tile_depths, tile_live, factor_b, factor_c, proj):
@@ -278,16 +312,17 @@
     slots = slot_total // owners
     rank = factor_b.shape[0]
     columns = proj.shape[1]
-    height = columns // owners
+    half = columns // 2
+    height = half // owners
     chunks_b, chunks_c = n_ia * n_ka, n_ia * n_ja
     vmem, dma = pltpu.VMEM, pltpu.SemaphoreType.DMA
     f32, bf16, i32 = jnp.float32, jnp.bfloat16, jnp.int32
-    return pl.pallas_call(
+    held = pl.pallas_call(
         functools.partial(kernel, n_ia, n_ja, n_ka),
         out_shape=(
-            jax.ShapeDtypeStruct((ROWS_DEV, columns), f32),
-            jax.ShapeDtypeStruct((columns, columns), f32),
-            jax.ShapeDtypeStruct((rank, ROWS_DEV), f32),
+            vmem((ROWS_DEV, columns), f32),
+            vmem((rank, ROWS_DEV), f32),
+            vmem((3, owners, height, half), bf16),
         ),
         in_specs=[pl.BlockSpec(memory_space=pl.ANY)] * 8,
         out_specs=tuple([pl.BlockSpec(memory_space=pltpu.VMEM)] * 3),
@@ -308,26 +343,37 @@
             vmem((owners, slots, 2 * rank, tile), bf16),
             vmem((owners, slots, 2 * rank, tile), bf16),
             vmem((columns, slots * tile), bf16),
-            vmem((owners, height, columns), f32),
-            vmem((owners, height, columns), bf16),
-            vmem((owners, height, columns), bf16),
-            vmem((height, columns), bf16),
-            vmem((n_ia, height, columns), bf16),
-            vmem((owners, height, columns), bf16),
+            vmem((columns, ROWS_DEV), f32),
+            vmem((3, owners, height, half), f32),
+            vmem((3, owners, height, half), bf16),
+            vmem((3, owners, height, half), bf16),
+            vmem((3, height, half), bf16),
+            vmem((3, n_ia, height, half), bf16),
             dma((8,)),
             dma((chunks_b,)), dma((chunks_b,)),
             dma((chunks_c,)), dma((chunks_c,)),
             dma((owners,)), dma((owners,)),
             dma((owners,)), dma((owners,)),
-            dma((owners,)), dma((owners,)),
-            dma((n_ia,)), dma((n_ia,)),
-            dma((owners,)), dma((owners,)),
+            dma((3, owners)), dma((3, owners)),
+            dma((3, n_ia)), dma((3, n_ia)),
+            dma((3, owners)), dma((3, owners)),
         ],
         compiler_params=pltpu.CompilerParams(collective_id=0, has_side_effects=True),
     )(
         tile_values, tile_rows, tile_cols, tile_depths, tile_live,
         factor_b[:, 0, :], factor_c[:, 0, :], proj,
     )
+    return pl.pallas_call(
+        finish,
+        out_shape=(
+            jax.ShapeDtypeStruct((ROWS_DEV, columns), f32),
+            jax.ShapeDtypeStruct((columns, columns), f32),
+            jax.ShapeDtypeStruct((rank, ROWS_DEV), f32),
+        ),
+        in_specs=[pl.BlockSpec(memory_space=pltpu.VMEM)] * 3,
+        out_specs=tuple([pl.BlockSpec(memory_space=pl.ANY)] * 3),
+        scratch_shapes=[vmem((columns, columns), f32), dma((4,))],
+    )(*(pltpu.with_memory_space_constraint(array, vmem) for array in held))
 
 
 def solution(mesh):

time: 34.7 us -> 31.4 us (0.905)
  local copies, waits for them, and re-layouts: 3.76 us -> 0 us
  Pallas kernels: 30.1 us -> 30.6 us
    unnamed x5 -> x0, local copies, waits for them, and re-layouts: 3.76 us -> none
    pallas_call x1 -> x2, Pallas kernels: 30.1 us -> 30.6 us  [the longest x1 29.9 us: on_device(): pl.pallas_call(functools.partial(kernel, n_ia, n_ja, n_ka), out_shape=(vm...]
where the time goes in v2:
time: 31.4 us; the launch traced here: 31.3 us
  Pallas kernels  30.6 us (97%)
  between operations  0.64 us (2%)
    pallas_call x1, Pallas kernels, on_device(): pl.pallas_call(functools.partial(kernel, n_ia, n_ja, n_ka), out_shape=(vm...  29.9 us
    pallas_call x1, Pallas kernels, on_device(): pl.pallas_call(finish, out_shape=(jax.ShapeDtypeStruct((ROWS_DEV, columns...  0.8 us

profile of v2, /device:TPU:0, one launch (start us, length us, event | category | flops | bytes accessed | tf_op | source)
XLA Modules:
  0.0 31.3 jit_solution(12513296979264792920)
XLA Ops:
  0.6 29.9 %shard_map.103 = (f32[64,256]{1,0:T(8,128)S(1)}, f32[16,64]{1,0:T(8,128)S(1)}, bf16[3,8,16,128]{3,2,1,0:T(8,128)(2,1)S(1)}) custom-call(bf16[24,128]{1,0:T(8,128)(2,1)} %values.1, s32[24,128]{1,0:T(8,128)} %rows.1, s32[24,128]{1,0:T(8,128)} %cols.1, s32[24,128]{1,0:T(8,128)} %depths.1, s32[1,8]{1,0:T(1,128)} %live.1, bf16[16,128]{1,0:T(8,128)(2,1)} %bitcast.2, ...), custom_call_target="tpu_custom_call" | custom-call | tf_op jit(solution)/shard_map/pallas_call | solution.py:320
  30.5 0.8 %shard_map.104 = (f32[64,256]{1,0:T(8,128)}, f32[256,256]{1,0:T(8,128)}, f32[16,64]{1,0:T(8,128)}) custom-call(f32[64,256]{1,0:T(8,128)S(1)} %get-tuple-element.6.y, f32[16,64]{1,0:T(8,128)S(1)} %get-tuple-element.7.nf, bf16[3,8,16,128]{3,2,1,0:T(8,128)(2,1)S(1)} %get-tuple-element.8.final), custom_call_target="tpu_custom_call" | custom-call | tf_op jit(solution)/shard_map/pallas_call | solution.py:366

commit v3 on v2

--- a/solution.py
+++ b/solution.py
@@ -10,6 +10,17 @@
 ROWS_DEV = 64
 LANES = 128
 MESH = pl.DeviceIdType.MESH
+
+
+def each(begin, end):
+    if end - begin > 16:
+        return pl.loop(begin, end)
+
+    def run(body):
+        for step in range(begin, end):
+            body(step)
+
+    return run
 
 
 def repeat(count, body, init):
@@ -46,7 +57,7 @@
     values_v, rows_v, cols_v, depths_v, proj_v, live_s, scale_v,
     tb_in, tc_in, tb, tc,
     rows_send, rows_recv, pay_send, pay_recv, kron,
-    yt_v, g_own, g_send, g_recv, z_send, z_recv,
+    yt_v, g_left, g_right, g_own, g_send, g_recv, z_send, z_recv,
     load_sem, tb_ssem, tb_rsem, tc_ssem, tc_rsem, rows_ssem, rows_rsem, pay_ssem, pay_rsem,
     g_ssem, g_rsem, z_ssem, z_rsem, f_ssem, f_rsem,
 ):
@@ -75,17 +86,34 @@
         return (peer // n_ja, lax.rem(peer, n_ja), c)
 
     def o_peer(j):
-        peer = lax.rem(me_o + j, owners)
-        return (a, peer // n_ka, lax.rem(peer, n_ka))
+        return (a, lax.rem(b + j // n_ka, n_ja), lax.rem(c + j % n_ka, n_ka))
+
+    def to_o(j):
+        return lax.rem(b + j // n_ka, n_ja) * n_ka + lax.rem(c + j % n_ka, n_ka)
+
+    def from_o(j):
+        return lax.rem(b + n_ja - j // n_ka, n_ja) * n_ka + lax.rem(c + n_ka - j % n_ka, n_ka)
 
     def a_peer(j):
         return (lax.rem(a + j, n_ia), b, c)
 
     barrier = pltpu.get_barrier_semaphore()
     for count, peer in ((n_ia * n_ka, b_peer), (n_ia * n_ja, c_peer), (owners, o_peer)):
-        @pl.loop(1, count)
+        @each(1, count)
         def _(j, peer=peer):
             pl.semaphore_signal(barrier, inc=1, device_id=peer(j), device_id_type=MESH)
+
+    for load in loads:
+        load.wait()
+
+    @each(0, owners)
+    def _(o):
+        for t in range(slots):
+            rows_send[o, pl.ds(t, 1), :] = rows_v[pl.ds(o * slots + t, 1), :]
+
+    scale_v[...] = values_v[...].astype(jnp.float32)
+    tb[me_b] = tb_in[me_b].astype(jnp.float32)
+    tc[me_c] = tc_in[me_c].astype(jnp.float32)
     pl.semaphore_wait(barrier, n_ia * n_ka + n_ia * n_ja + owners - 3)
 
     def remote(src, dst, ssem, rsem, peer):
@@ -100,49 +128,37 @@
     def tc_copy(j, slot):
         return remote(fc, tc_in.at[slot], tc_ssem.at[j], tc_rsem.at[slot], c_peer(j))
 
-    @pl.loop(1, n_ia * n_ka)
+    @each(1, n_ia * n_ka)
     def _(j):
         tb_copy(j, me_b).start()
 
-    @pl.loop(1, n_ia * n_ja)
+    @each(1, n_ia * n_ja)
     def _(j):
         tc_copy(j, me_c).start()
-
-    for load in loads:
-        load.wait()
 
     def rows_copy(j, slot):
         return remote(
-            rows_send.at[lax.rem(me_o + j, owners)], rows_recv.at[slot],
+            rows_send.at[to_o(j)], rows_recv.at[slot],
             rows_ssem.at[j], rows_rsem.at[slot], o_peer(j),
         )
 
     def pay_copy(j, slot):
         return remote(
-            pay_send.at[lax.rem(me_o + j, owners)], pay_recv.at[slot],
+            pay_send.at[to_o(j)], pay_recv.at[slot],
             pay_ssem.at[j], pay_rsem.at[slot], o_peer(j),
         )
 
-    @pl.loop(0, owners)
-    def _(o):
-        for t in range(slots):
-            rows_send[o, pl.ds(t, 1), :] = rows_v[pl.ds(o * slots + t, 1), :]
-
-    @pl.loop(1, owners)
+    @each(1, owners)
     def _(j):
         rows_copy(j, me_o).start()
 
-    scale_v[...] = values_v[...].astype(jnp.float32)
-    tb[me_b] = tb_in[me_b].astype(jnp.float32)
-    tc[me_c] = tc_in[me_c].astype(jnp.float32)
-
-    @pl.loop(1, n_ia * n_ka)
+    @each(1, n_ia * n_ka)
     def _(j):
         slot = lax.rem(me_b + n_ia * n_ka - j, n_ia * n_ka)
         tb_copy(j, slot).wait_recv()
         tb[slot] = tb_in[slot].astype(jnp.float32)
 
-    @pl.loop(1, n_ia * n_ja)
+    @each(1, n_ia * n_ja)
     def _(j):
         slot = lax.rem(me_c + n_ia * n_ja - j, n_ia * n_ja)
         tc_copy(j, slot).wait_recv()
@@ -158,8 +174,8 @@
 
     @pl.loop(1, owners)
     def _(j):
-        fill(lax.rem(me_o + j, owners))
-        pay_copy(j, me_o).start()
+        fill(to_o(owners - j))
+        pay_copy(owners - j, me_o).start()
 
     fill(me_o)
 
@@ -181,28 +197,28 @@
 
     yt_v[...] = block(pay_send.at[me_o], rows_send.at[me_o])
 
-    @pl.loop(1, n_ia * n_ka)
+    @each(1, n_ia * n_ka)
     def _(j):
         tb_copy(j, me_b).wait_send()
 
-    @pl.loop(1, n_ia * n_ja)
+    @each(1, n_ia * n_ja)
     def _(j):
         tc_copy(j, me_c).wait_send()
 
+    @each(1, owners)
+    def _(j):
+        rows_copy(j, me_o).wait_send()
+
     @pl.loop(1, owners)
     def _(j):
-        rows_copy(j, me_o).wait_send()
-
-    @pl.loop(1, owners)
-    def _(j):
-        slot = lax.rem(me_o + owners - j, owners)
+        slot = from_o(j)
         rows_copy(j, slot).wait_recv()
         pay_copy(j, slot).wait_recv()
         yt_v[...] += block(pay_recv.at[slot], rows_recv.at[slot])
 
     def g_copy(i, j, slot):
         return remote(
-            g_send.at[i, lax.rem(me_o + j, owners)], g_recv.at[i, slot],
+            g_send.at[i, to_o(j)], g_recv.at[i, slot],
             g_ssem.at[i, j], g_rsem.at[i, slot], o_peer(j),
         )
 
@@ -216,19 +232,23 @@
 
     half = kron.shape[0] // 2
     pieces = ((0, 0), (0, 1), (1, 1))
+    yt = yt_v[...]
+    high = yt.astype(jnp.bfloat16).astype(jnp.float32)
+    low = yt - high
+    g_left[...] = jnp.concatenate([high, low, high, low], axis=1).astype(jnp.bfloat16)
+    g_right[...] = jnp.concatenate([high, high, low, low], axis=1).astype(jnp.bfloat16)
     scale = 1.0 / (ROWS_DEV * owners * n_ia)
     for i, (left, right) in enumerate(pieces):
         piece = lax.dot_general(
-            yt_v[pl.ds(left * half, half), :], yt_v[pl.ds(right * half, half), :],
-            (((1,), (1,)), ((), ())),
-            precision=lax.Precision.HIGHEST, preferred_element_type=jnp.float32,
+            g_left[pl.ds(left * half, half), :], g_right[pl.ds(right * half, half), :],
+            (((1,), (1,)), ((), ())), preferred_element_type=jnp.float32,
         ) * scale
         g_own[i] = piece.reshape(g_own.shape[1:])
         g_send[i] = piece.reshape(g_own.shape[1:]).astype(jnp.bfloat16)
 
-        @pl.loop(1, owners)
+        @each(1, owners)
         def _(j, i=i):
-            g_copy(i, j, me_o).start()
+            g_copy(i, owners - j, me_o).start()
 
     nf_out[...] = lax.dot_general(
         proj_v[...], yt_v[...], (((1,), (0,)), ((), ())),
@@ -236,14 +256,14 @@
     )
     y_out[...] = jnp.transpose(yt_v[...])
 
-    @pl.loop(1, owners)
+    @each(1, owners)
     def _(j):
         pay_copy(j, me_o).wait_send()
 
     for i in range(len(pieces)):
         total = g_own[i, me_o]
         for j in range(1, owners):
-            slot = lax.rem(me_o + owners - j, owners)
+            slot = from_o(j)
             g_copy(i, j, slot).wait_recv()
             total = total + g_recv[i, slot].astype(jnp.float32)
         z_send[i] = total.astype(jnp.bfloat16)
@@ -259,11 +279,11 @@
             total = total + z_recv[i, index].astype(jnp.float32)
         final[i, me_o] = total.astype(jnp.bfloat16)
 
-        @pl.loop(1, owners)
+        @each(1, owners)
         def _(j, i=i):
-            f_copy(i, j, me_o).start()
-
-    @pl.loop(1, owners)
+            f_copy(i, owners - j, me_o).start()
+
+    @each(1, owners)
     def _(j):
         for i in range(len(pieces)):
             g_copy(i, j, me_o).wait_send()
@@ -272,12 +292,12 @@
         for j in range(1, n_ia):
             z_copy(i, j, a).wait_send()
 
-    @pl.loop(1, owners)
+    @each(1, owners)
     def _(j):
         for i in range(len(pieces)):
-            f_copy(i, j, lax.rem(me_o + owners - j, owners)).wait_recv()
-
-    @pl.loop(1, owners)
+            f_copy(i, j, from_o(j)).wait_recv()
+
+    @each(1, owners)
     def _(j):
         for i in range(len(pieces)):
             f_copy(i, j, me_o).wait_send()
@@ -344,6 +364,8 @@
             vmem((owners, slots, 2 * rank, tile), bf16),
             vmem((columns, slots * tile), bf16),
             vmem((columns, ROWS_DEV), f32),
+            vmem((columns, 4 * ROWS_DEV), bf16),
+            vmem((columns, 4 * ROWS_DEV), bf16),
             vmem((3, owners, height, half), f32),
             vmem((3, owners, height, half), bf16),
             vmem((3, owners, height, half), bf16),

time: 31.4 us -> 30.8 us (0.981)
  Pallas kernels: 30.6 us -> 30 us
    pallas_call x1, Pallas kernels: 29.9 us -> 29.2 us  [on_device(): pl.pallas_call(functools.partial(kernel, n_ia, n_ja, n_ka), out_shape=(vm...]
where the time goes in v3:
time: 30.8 us; the launch traced here: 30.6 us
  Pallas kernels  30 us (97%)
  between operations  0.64 us (2%)
    pallas_call x1, Pallas kernels, on_device(): pl.pallas_call(functools.partial(kernel, n_ia, n_ja, n_ka), out_shape=(vm...  29.2 us
    pallas_call x1, Pallas kernels, on_device(): pl.pallas_call(finish, out_shape=(jax.ShapeDtypeStruct((ROWS_DEV, columns...  0.8 us

profile of v3, /device:TPU:0, one launch (start us, length us, event | category | flops | bytes accessed | tf_op | source)
XLA Modules:
  0.0 30.6 jit_solution(7322978965811453045)
XLA Ops:
  0.6 29.2 %shard_map.103 = (f32[64,256]{1,0:T(8,128)S(1)}, f32[16,64]{1,0:T(8,128)S(1)}, bf16[3,8,16,128]{3,2,1,0:T(8,128)(2,1)S(1)}) custom-call(bf16[24,128]{1,0:T(8,128)(2,1)} %values.1, s32[24,128]{1,0:T(8,128)} %rows.1, s32[24,128]{1,0:T(8,128)} %cols.1, s32[24,128]{1,0:T(8,128)} %depths.1, s32[1,8]{1,0:T(1,128)} %live.1, bf16[16,128]{1,0:T(8,128)(2,1)} %bitcast.2, ...), custom_call_target="tpu_custom_call" | custom-call | tf_op jit(solution)/shard_map/pallas_call | solution.py:340
  29.8 0.8 %shard_map.104 = (f32[64,256]{1,0:T(8,128)}, f32[256,256]{1,0:T(8,128)}, f32[16,64]{1,0:T(8,128)}) custom-call(f32[64,256]{1,0:T(8,128)S(1)} %get-tuple-element.6.y, f32[16,64]{1,0:T(8,128)S(1)} %get-tuple-element.7.nf, bf16[3,8,16,128]{3,2,1,0:T(8,128)(2,1)S(1)} %get-tuple-element.8.final), custom_call_target="tpu_custom_call" | custom-call | tf_op jit(solution)/shard_map/pallas_call | solution.py:388

commit v4 on v3

--- a/solution.py
+++ b/solution.py
@@ -69,6 +69,32 @@
     me_c = a * n_ja + b
     me_o = b * n_ka + c
 
+    def b_peer(j):
+        peer = lax.rem(me_b + j, n_ia * n_ka)
+        return (peer // n_ka, b, lax.rem(peer, n_ka))
+
+    def c_peer(j):
+        peer = lax.rem(me_c + j, n_ia * n_ja)
+        return (peer // n_ja, lax.rem(peer, n_ja), c)
+
+    def o_peer(j):
+        return (a, lax.rem(b + j // n_ka, n_ja), lax.rem(c + j % n_ka, n_ka))
+
+    def to_o(j):
+        return lax.rem(b + j // n_ka, n_ja) * n_ka + lax.rem(c + j % n_ka, n_ka)
+
+    def from_o(j):
+        return lax.rem(b + n_ja - j // n_ka, n_ja) * n_ka + lax.rem(c + n_ka - j % n_ka, n_ka)
+
+    def a_peer(j):
+        return (lax.rem(a + j, n_ia), b, c)
+
+    barrier = pltpu.get_barrier_semaphore()
+    for count, peer in ((n_ia * n_ka, b_peer), (n_ia * n_ja, c_peer), (owners, o_peer)):
+        @each(1, count)
+        def _(j, peer=peer):
+            pl.semaphore_signal(barrier, inc=1, device_id=peer(j), device_id_type=MESH)
+
     loads = []
     for index, (src, dst) in enumerate((
         (values, values_v), (rows, rows_v), (cols, cols_v), (depths, depths_v),
@@ -77,31 +103,27 @@
         loads.append(pltpu.make_async_copy(src, dst, load_sem.at[index]))
         loads[-1].start()
 
-    def b_peer(j):
-        peer = lax.rem(me_b + j, n_ia * n_ka)
-        return (peer // n_ka, b, lax.rem(peer, n_ka))
-
-    def c_peer(j):
-        peer = lax.rem(me_c + j, n_ia * n_ja)
-        return (peer // n_ja, lax.rem(peer, n_ja), c)
-
-    def o_peer(j):
-        return (a, lax.rem(b + j // n_ka, n_ja), lax.rem(c + j % n_ka, n_ka))
-
-    def to_o(j):
-        return lax.rem(b + j // n_ka, n_ja) * n_ka + lax.rem(c + j % n_ka, n_ka)
-
-    def from_o(j):
-        return lax.rem(b + n_ja - j // n_ka, n_ja) * n_ka + lax.rem(c + n_ka - j % n_ka, n_ka)
-
-    def a_peer(j):
-        return (lax.rem(a + j, n_ia), b, c)
-
-    barrier = pltpu.get_barrier_semaphore()
-    for count, peer in ((n_ia * n_ka, b_peer), (n_ia * n_ja, c_peer), (owners, o_peer)):
-        @each(1, count)
-        def _(j, peer=peer):
-            pl.semaphore_signal(barrier, inc=1, device_id=peer(j), device_id_type=MESH)
+    pl.semaphore_wait(barrier, n_ia * n_ka + n_ia * n_ja + owners - 3)
+
+    def remote(src, dst, ssem, rsem, peer):
+        return pltpu.make_async_remote_copy(
+            src_ref=src, dst_ref=dst, send_sem=ssem, recv_sem=rsem,
+            device_id=peer, device_id_type=MESH,
+        )
+
+    def tb_copy(j, slot):
+        return remote(fb, tb_in.at[slot], tb_ssem.at[j], tb_rsem.at[slot], b_peer(j))
+
+    def tc_copy(j, slot):
+        return remote(fc, tc_in.at[slot], tc_ssem.at[j], tc_rsem.at[slot], c_peer(j))
+
+    @each(1, n_ia * n_ka)
+    def _(j):
+        tb_copy(j, me_b).start()
+
+    @each(1, n_ia * n_ja)
+    def _(j):
+        tc_copy(j, me_c).start()
 
     for load in loads:
         load.wait()
@@ -114,27 +136,6 @@
     scale_v[...] = values_v[...].astype(jnp.float32)
     tb[me_b] = tb_in[me_b].astype(jnp.float32)
     tc[me_c] = tc_in[me_c].astype(jnp.float32)
-    pl.semaphore_wait(barrier, n_ia * n_ka + n_ia * n_ja + owners - 3)
-
-    def remote(src, dst, ssem, rsem, peer):
-        return pltpu.make_async_remote_copy(
-            src_ref=src, dst_ref=dst, send_sem=ssem, recv_sem=rsem,
-            device_id=peer, device_id_type=MESH,
-        )
-
-    def tb_copy(j, slot):
-        return remote(fb, tb_in.at[slot], tb_ssem.at[j], tb_rsem.at[slot], b_peer(j))
-
-    def tc_copy(j, slot):
-        return remote(fc, tc_in.at[slot], tc_ssem.at[j], tc_rsem.at[slot], c_peer(j))
-
-    @each(1, n_ia * n_ka)
-    def _(j):
-        tb_copy(j, me_b).start()
-
-    @each(1, n_ia * n_ja)
-    def _(j):
-        tc_copy(j, me_c).start()
 
     def rows_copy(j, slot):
         return remote(
@@ -216,18 +217,17 @@
         pay_copy(j, slot).wait_recv()
         yt_v[...] += block(pay_recv.at[slot], rows_recv.at[slot])
 
-    def g_copy(i, j, slot):
+    def g_copy(j, slot):
         return remote(
-            g_send.at[i, to_o(j)], g_recv.at[i, slot],
-            g_ssem.at[i, j], g_rsem.at[i, slot], o_peer(j),
-        )
-
-    def z_copy(i, j, slot):
-        return remote(z_send.at[i], z_recv.at[i, slot], z_ssem.at[i, j], z_rsem.at[i, slot], a_peer(j))
-
-    def f_copy(i, j, slot):
+            g_send.at[:, to_o(j)], g_recv.at[:, slot], g_ssem.at[j], g_rsem.at[slot], o_peer(j)
+        )
+
+    def z_copy(j, slot):
+        return remote(z_send, z_recv.at[slot], z_ssem.at[j], z_rsem.at[slot], a_peer(j))
+
+    def f_copy(j, slot):
         return remote(
-            final.at[i, slot], final.at[i, slot], f_ssem.at[i, j], f_rsem.at[i, slot], o_peer(j)
+            final.at[:, slot], final.at[:, slot], f_ssem.at[j], f_rsem.at[slot], o_peer(j)
         )
 
     half = kron.shape[0] // 2
@@ -246,9 +246,9 @@
         g_own[i] = piece.reshape(g_own.shape[1:])
         g_send[i] = piece.reshape(g_own.shape[1:]).astype(jnp.bfloat16)
 
-        @each(1, owners)
-        def _(j, i=i):
-            g_copy(i, owners - j, me_o).start()
+    @each(1, owners)
+    def _(j):
+        g_copy(owners - j, me_o).start()
 
     nf_out[...] = lax.dot_general(
         proj_v[...], yt_v[...], (((1,), (0,)), ((), ())),
@@ -260,47 +260,41 @@
     def _(j):
         pay_copy(j, me_o).wait_send()
 
-    for i in range(len(pieces)):
-        total = g_own[i, me_o]
-        for j in range(1, owners):
-            slot = from_o(j)
-            g_copy(i, j, slot).wait_recv()
-            total = total + g_recv[i, slot].astype(jnp.float32)
-        z_send[i] = total.astype(jnp.bfloat16)
-        z_recv[i, a] = total.astype(jnp.bfloat16)
-        for j in range(1, n_ia):
-            z_copy(i, j, a).start()
-
-    for i in range(len(pieces)):
-        for j in range(1, n_ia):
-            z_copy(i, j, lax.rem(a + n_ia - j, n_ia)).wait_recv()
-        total = z_recv[i, 0].astype(jnp.float32)
-        for index in range(1, n_ia):
-            total = total + z_recv[i, index].astype(jnp.float32)
-        final[i, me_o] = total.astype(jnp.bfloat16)
-
-        @each(1, owners)
-        def _(j, i=i):
-            f_copy(i, owners - j, me_o).start()
-
-    @each(1, owners)
-    def _(j):
-        for i in range(len(pieces)):
-            g_copy(i, j, me_o).wait_send()
-
-    for i in range(len(pieces)):
-        for j in range(1, n_ia):
-            z_copy(i, j, a).wait_send()
-
-    @each(1, owners)
-    def _(j):
-        for i in range(len(pieces)):
-            f_copy(i, j, from_o(j)).wait_recv()
-
-    @each(1, owners)
-    def _(j):
-        for i in range(len(pieces)):
-            f_copy(i, j, me_o).wait_send()
+    total = g_own[:, me_o]
+    for j in range(1, owners):
+        slot = from_o(j)
+        g_copy(j, slot).wait_recv()
+        total = total + g_recv[:, slot].astype(jnp.float32)
+    z_send[...] = total.astype(jnp.bfloat16)
+    for j in range(1, n_ia):
+        z_copy(j, a).start()
+    z_recv[a] = total.astype(jnp.bfloat16)
+
+    for j in range(1, n_ia):
+        z_copy(j, lax.rem(a + n_ia - j, n_ia)).wait_recv()
+    total = z_recv[0].astype(jnp.float32)
+    for index in range(1, n_ia):
+        total = total + z_recv[index].astype(jnp.float32)
+    final[:, me_o] = total.astype(jnp.bfloat16)
+
+    @each(1, owners)
+    def _(j):
+        f_copy(owners - j, me_o).start()
+
+    @each(1, owners)
+    def _(j):
+        g_copy(j, me_o).wait_send()
+
+    for j in range(1, n_ia):
+        z_copy(j, a).wait_send()
+
+    @each(1, owners)
+    def _(j):
+        f_copy(j, from_o(j)).wait_recv()
+
+    @each(1, owners)
+    def _(j):
+        f_copy(j, me_o).wait_send()
 
 
 def finish(y, nf, final, y_out, gram_out, nf_out, gram_v, sem):
@@ -370,15 +364,15 @@
             vmem((3, owners, height, half), bf16),
             vmem((3, owners, height, half), bf16),
             vmem((3, height, half), bf16),
-            vmem((3, n_ia, height, half), bf16),
+            vmem((n_ia, 3, height, half), bf16),
             dma((8,)),
             dma((chunks_b,)), dma((chunks_b,)),
             dma((chunks_c,)), dma((chunks_c,)),
             dma((owners,)), dma((owners,)),
             dma((owners,)), dma((owners,)),
-            dma((3, owners)), dma((3, owners)),
-            dma((3, n_ia)), dma((3, n_ia)),
-            dma((3, owners)), dma((3, owners)),
+            dma((owners,)), dma((owners,)),
+            dma((n_ia,)), dma((n_ia,)),
+            dma((owners,)), dma((owners,)),
         ],
         compiler_params=pltpu.CompilerParams(collective_id=0, has_side_effects=True),
     )(

time: 30.8 us -> 30.3 us (0.984)
  Pallas kernels: 30 us -> 29.5 us
    pallas_call x1, Pallas kernels: 29.2 us -> 28.7 us  [on_device(): pl.pallas_call(functools.partial(kernel, n_ia, n_ja, n_ka), out_shape=(vm...]
where the time goes in v4:
time: 30.3 us; the launch traced here: 30.2 us
  Pallas kernels  29.5 us (97%)
  between operations  0.64 us (2%)
    pallas_call x1, Pallas kernels, on_device(): pl.pallas_call(functools.partial(kernel, n_ia, n_ja, n_ka), out_shape=(vm...  28.7 us
    pallas_call x1, Pallas kernels, on_device(): pl.pallas_call(finish, out_shape=(jax.ShapeDtypeStruct((ROWS_DEV, columns...  0.8 us

profile of v4, /device:TPU:0, one launch (start us, length us, event | category | flops | bytes accessed | tf_op | source)
XLA Modules:
  0.0 30.2 jit_solution(4083569705088467739)
XLA Ops:
  0.6 28.7 %shard_map.103 = (f32[64,256]{1,0:T(8,128)S(1)}, f32[16,64]{1,0:T(8,128)S(1)}, bf16[3,8,16,128]{3,2,1,0:T(8,128)(2,1)S(1)}) custom-call(bf16[24,128]{1,0:T(8,128)(2,1)} %values.1, s32[24,128]{1,0:T(8,128)} %rows.1, s32[24,128]{1,0:T(8,128)} %cols.1, s32[24,128]{1,0:T(8,128)} %depths.1, s32[1,8]{1,0:T(1,128)} %live.1, bf16[16,128]{1,0:T(8,128)(2,1)} %bitcast.2, ...), custom_call_target="tpu_custom_call" | custom-call | tf_op jit(solution)/shard_map/pallas_call | solution.py:334
  29.4 0.8 %shard_map.104 = (f32[64,256]{1,0:T(8,128)}, f32[256,256]{1,0:T(8,128)}, f32[16,64]{1,0:T(8,128)}) custom-call(f32[64,256]{1,0:T(8,128)S(1)} %get-tuple-element.6.y, f32[16,64]{1,0:T(8,128)S(1)} %get-tuple-element.7.nf, bf16[3,8,16,128]{3,2,1,0:T(8,128)(2,1)S(1)} %get-tuple-element.8.final), custom_call_target="tpu_custom_call" | custom-call | tf_op jit(solution)/shard_map/pallas_call | solution.py:382

commit v5 on v4

--- a/solution.py
+++ b/solution.py
@@ -117,13 +117,13 @@
     def tc_copy(j, slot):
         return remote(fc, tc_in.at[slot], tc_ssem.at[j], tc_rsem.at[slot], c_peer(j))
 
+    @each(1, n_ia * n_ja)
+    def _(j):
+        tc_copy(n_ia * n_ja - j, me_c).start()
+
     @each(1, n_ia * n_ka)
     def _(j):
-        tb_copy(j, me_b).start()
-
-    @each(1, n_ia * n_ja)
-    def _(j):
-        tc_copy(j, me_c).start()
+        tb_copy(n_ia * n_ka - j, me_b).start()
 
     for load in loads:
         load.wait()

time: 30.3 us -> 30 us (0.990)
    pallas_call x1, Pallas kernels: 28.7 us -> 28.4 us  [on_device(): pl.pallas_call(functools.partial(kernel, n_ia, n_ja, n_ka), out_shape=(vm...]
where the time goes in v5:
time: 30 us; the launch traced here: 29.8 us
  Pallas kernels  29.2 us (97%)
  between operations  0.64 us (2%)
    pallas_call x1, Pallas kernels, on_device(): pl.pallas_call(functools.partial(kernel, n_ia, n_ja, n_ka), out_shape=(vm...  28.4 us
    pallas_call x1, Pallas kernels, on_device(): pl.pallas_call(finish, out_shape=(jax.ShapeDtypeStruct((ROWS_DEV, columns...  0.8 us

profile of v5, /device:TPU:0, one launch (start us, length us, event | category | flops | bytes accessed | tf_op | source)
XLA Modules:
  0.0 29.8 jit_solution(10373694812185659593)
XLA Ops:
  0.6 28.4 %shard_map.103 = (f32[64,256]{1,0:T(8,128)S(1)}, f32[16,64]{1,0:T(8,128)S(1)}, bf16[3,8,16,128]{3,2,1,0:T(8,128)(2,1)S(1)}) custom-call(bf16[24,128]{1,0:T(8,128)(2,1)} %values.1, s32[24,128]{1,0:T(8,128)} %rows.1, s32[24,128]{1,0:T(8,128)} %cols.1, s32[24,128]{1,0:T(8,128)} %depths.1, s32[1,8]{1,0:T(1,128)} %live.1, bf16[16,128]{1,0:T(8,128)(2,1)} %bitcast.2, ...), custom_call_target="tpu_custom_call" | custom-call | tf_op jit(solution)/shard_map/pallas_call | solution.py:334
  29.0 0.8 %shard_map.104 = (f32[64,256]{1,0:T(8,128)}, f32[256,256]{1,0:T(8,128)}, f32[16,64]{1,0:T(8,128)}) custom-call(f32[64,256]{1,0:T(8,128)S(1)} %get-tuple-element.6.y, f32[16,64]{1,0:T(8,128)S(1)} %get-tuple-element.7.nf, bf16[3,8,16,128]{3,2,1,0:T(8,128)(2,1)S(1)} %get-tuple-element.8.final), custom_call_target="tpu_custom_call" | custom-call | tf_op jit(solution)/shard_map/pallas_call | solution.py:382

commit v6 on v5

--- a/solution.py
+++ b/solution.py
@@ -92,8 +92,8 @@
     barrier = pltpu.get_barrier_semaphore()
     for count, peer in ((n_ia * n_ka, b_peer), (n_ia * n_ja, c_peer), (owners, o_peer)):
         @each(1, count)
-        def _(j, peer=peer):
-            pl.semaphore_signal(barrier, inc=1, device_id=peer(j), device_id_type=MESH)
+        def _(j, peer=peer, count=count):
+            pl.semaphore_signal(barrier, inc=1, device_id=peer(count - j), device_id_type=MESH)
 
     loads = []
     for index, (src, dst) in enumerate((
@@ -266,7 +266,7 @@
         g_copy(j, slot).wait_recv()
         total = total + g_recv[:, slot].astype(jnp.float32)
     z_send[...] = total.astype(jnp.bfloat16)
-    for j in range(1, n_ia):
+    for j in range(n_ia - 1, 0, -1):
         z_copy(j, a).start()
     z_recv[a] = total.astype(jnp.bfloat16)
 

time: 30 us -> 30.3 us (1.010)
    pallas_call x1, Pallas kernels: 28.4 us -> 28.7 us  [on_device(): pl.pallas_call(functools.partial(kernel, n_ia, n_ja, n_ka), out_shape=(vm...]
where the time goes in v6:
time: 30.3 us; the launch traced here: 30.2 us
  Pallas kernels  29.5 us (97%)
  between operations  0.64 us (2%)
    pallas_call x1, Pallas kernels, on_device(): pl.pallas_call(functools.partial(kernel, n_ia, n_ja, n_ka), out_shape=(vm...  28.7 us
    pallas_call x1, Pallas kernels, on_device(): pl.pallas_call(finish, out_shape=(jax.ShapeDtypeStruct((ROWS_DEV, columns...  0.8 us

profile of v6, /device:TPU:0, one launch (start us, length us, event | category | flops | bytes accessed | tf_op | source)
XLA Modules:
  0.0 30.2 jit_solution(8643788563968941959)
XLA Ops:
  0.6 28.7 %shard_map.103 = (f32[64,256]{1,0:T(8,128)S(1)}, f32[16,64]{1,0:T(8,128)S(1)}, bf16[3,8,16,128]{3,2,1,0:T(8,128)(2,1)S(1)}) custom-call(bf16[24,128]{1,0:T(8,128)(2,1)} %values.1, s32[24,128]{1,0:T(8,128)} %rows.1, s32[24,128]{1,0:T(8,128)} %cols.1, s32[24,128]{1,0:T(8,128)} %depths.1, s32[1,8]{1,0:T(1,128)} %live.1, bf16[16,128]{1,0:T(8,128)(2,1)} %bitcast.2, ...), custom_call_target="tpu_custom_call" | custom-call | tf_op jit(solution)/shard_map/pallas_call | solution.py:334
  29.4 0.8 %shard_map.104 = (f32[64,256]{1,0:T(8,128)}, f32[256,256]{1,0:T(8,128)}, f32[16,64]{1,0:T(8,128)}) custom-call(f32[64,256]{1,0:T(8,128)S(1)} %get-tuple-element.6.y, f32[16,64]{1,0:T(8,128)S(1)} %get-tuple-element.7.nf, bf16[3,8,16,128]{3,2,1,0:T(8,128)(2,1)S(1)} %get-tuple-element.8.final), custom_call_target="tpu_custom_call" | custom-call | tf_op jit(solution)/shard_map/pallas_call | solution.py:382
